TPU v7x, 32 devices: a whole 2x2x4 slice. The times are simulated.
32 devices in a mesh: dp: 4 (over y, core), fsdp: 4 (over z), tensor: 2 (over x).
Axes of the slice: x: 2, y: 2, z: 4, core: 2. Of those that a mesh axis runs over, the one named last changes fastest.
Arguments:
- hidden_in: bfloat16 [7168, 8192], P(('dp', 'fsdp')), may hold values from -6 to 6
- queries: bfloat16 [7168, 8192], P(('dp', 'fsdp'), 'tensor')
- keys: bfloat16 [7168, 1024], P(('dp', 'fsdp'), 'tensor')
- output_gradient: bfloat16 [7168, 8192], P(('dp', 'fsdp'), 'tensor'), may hold values from -6 to 6
- rewards: float32 [16], P(('dp', 'fsdp')), may hold values from 0 to 4
- lengths: int32 [16], P(('dp', 'fsdp')), may hold values from 112 to 448
- master: float32 [8192, 1024], P(('dp', 'fsdp'), 'tensor'), may hold values from -0.0625 to 0.0625
- moment: float32 [8192, 1024], P(('dp', 'fsdp'), 'tensor'), may hold values from -6 to 6
- adam_second_moment: float32 [8192, 1024], P(('dp', 'fsdp'), 'tensor'), may hold values from 0.25 to 4
- layout: int32 [8], replicated, may hold values from 0 to 7, each once
Outputs:
- updated_master_weight: float32 [8192, 1024], P(('dp', 'fsdp'), 'tensor')
- new_moment: float32 [8192, 1024], P(('dp', 'fsdp'), 'tensor')
- new_second: float32 [8192, 1024], P(('dp', 'fsdp'), 'tensor')
- rollout_value_weight: bfloat16 [8192, 1024], P(('dp', 'fsdp'), 'tensor')
All inputs are finite; a program needn't handle non-finite values.
Results may differ from a plain program's by a relative error of at most 0.0014.
Values may be sent and summed in bfloat16 or wider, within the bound.
A program may use at most 192 MiB of HBM per device.

v0:
```python
import jax
import jax.numpy as jnp
from jax import lax
from jax.sharding import PartitionSpec as P

HEAD_SIZE = 128
QUERY_PER_VALUE = 8


def value_grad(query_matrix, key_matrix, out_rows, value_weight, length):
    token_slot_index = query_matrix.shape[0]
    heads_local = key_matrix.shape[1] // HEAD_SIZE
    query_head_rows = query_matrix.reshape(
        token_slot_index, heads_local, QUERY_PER_VALUE, HEAD_SIZE
    )
    key_head_rows = key_matrix.reshape(token_slot_index, heads_local, HEAD_SIZE)
    scores = jnp.einsum(
        "tkgd,skd->kgts", query_head_rows, key_head_rows, preferred_element_type=jnp.float32
    ) / jnp.sqrt(jnp.float32(HEAD_SIZE))
    position = jnp.arange(token_slot_index)
    allowed = (position[None, :] <= position[:, None]) & (position[None, :] < length)
    scores = jnp.where(allowed[None, None], scores, jnp.float32(-1e30))
    top = jnp.max(scores, axis=-1, keepdims=True)
    expo = jnp.exp(scores - top)
    probs = (expo / jnp.sum(expo, axis=-1, keepdims=True)).astype(jnp.bfloat16)
    attention_gradient = (value_weight[:, None] * out_rows.astype(jnp.float32)).astype(jnp.bfloat16)
    head_gradient = attention_gradient.reshape(
        token_slot_index, heads_local, QUERY_PER_VALUE, HEAD_SIZE
    )
    value_gradient = jnp.einsum(
        "kgts,tkgd->skd", probs, head_gradient, preferred_element_type=jnp.float32
    )
    return value_gradient.reshape(token_slot_index, heads_local * HEAD_SIZE).astype(jnp.bfloat16)


def on_device(
    hidden_in,
    queries,
    keys,
    output_gradient,
    rewards,
    lengths,
    master,
    moment,
    adam_second_moment,
    layout,
):
    reward_sum, length_sum = lax.psum(
        (jnp.sum(rewards), jnp.sum(lengths).astype(jnp.float32)), ("dp", "fsdp")
    )
    seq_count = jnp.float32(lax.axis_size(("dp", "fsdp")))
    advantage = rewards[0] - reward_sum / seq_count
    position = jnp.arange(hidden_in.shape[0])
    value_weight = jnp.where(
        position < lengths[0], advantage * seq_count / length_sum, jnp.float32(0.0)
    )
    value_gradient = value_grad(queries, keys, output_gradient, value_weight, lengths[0])
    grad = lax.psum_scatter(
        lax.dot_general(
            hidden_in, value_gradient, (((0,), (0,)), ((), ())), preferred_element_type=jnp.float32
        ),
        ("dp", "fsdp"),
        scatter_dimension=0,
        tiled=True,
    )
    new_moment = 0.9 * moment + 0.1 * grad
    new_second = 0.95 * adam_second_moment + 0.05 * grad * grad
    corrected = new_moment / (1.0 - 0.9**10) / (jnp.sqrt(new_second / (1.0 - 0.95**10)) + 1e-08)
    updated_master_weight = master - 0.002 * (corrected + 0.1 * master)
    rounded_weight = updated_master_weight.astype(jnp.bfloat16)
    row_count = rounded_weight.shape[0]
    heads_local = rounded_weight.shape[1] // HEAD_SIZE
    targets = lax.dynamic_slice_in_dim(layout, lax.axis_index("tensor") * heads_local, heads_local)
    piece = lax.all_gather(rounded_weight, "tensor", axis=1, tiled=True)
    piece_heads = piece.shape[1] // HEAD_SIZE
    piece_rows = piece.reshape(row_count, piece_heads, HEAD_SIZE)
    carry_rows = jnp.zeros_like(rounded_weight).reshape(row_count, heads_local, HEAD_SIZE)
    chosen = []
    for slot in range(heads_local):
        wanted = targets[slot]
        inside = (wanted >= 0) & (wanted < piece_heads)
        offset = jnp.clip(wanted, 0, piece_heads - 1)
        candidate = lax.dynamic_index_in_dim(piece_rows, offset, 1, keepdims=False)
        chosen.append(jnp.where(inside, candidate, carry_rows[:, slot]))
    rollout_value_weight = jnp.stack(chosen, axis=1).reshape(row_count, heads_local * HEAD_SIZE)
    return (updated_master_weight, new_moment, new_second, rollout_value_weight)


def solution(mesh):
    placed = (
        P(("dp", "fsdp"), None),
        P(("dp", "fsdp"), "tensor"),
        P(("dp", "fsdp"), "tensor"),
        P(("dp", "fsdp"), "tensor"),
        P(("dp", "fsdp")),
        P(("dp", "fsdp")),
        P(("dp", "fsdp"), "tensor"),
        P(("dp", "fsdp"), "tensor"),
        P(("dp", "fsdp"), "tensor"),
        P(),
    )
    return jax.shard_map(
        on_device,
        mesh=mesh,
        in_specs=placed,
        out_specs=(
            P(("dp", "fsdp"), "tensor"),
            P(("dp", "fsdp"), "tensor"),
            P(("dp", "fsdp"), "tensor"),
            P(("dp", "fsdp"), "tensor"),
        ),
        check_vma=False,
    )
```

profile of v0, /device:TPU:0, one launch (start us, length us, event | category | flops | bytes accessed | tf_op | source)
XLA Modules:
  0.0 377.8 jit_solution(9101465570995655895)
XLA Ops:
  7.2 0.0 copy-start.4
  7.2 0.0 reduce-scatter.2.cloned.1.call-start
  8.6 35.8 %all-reduce = (f32[]{:T(128)}, f32[]{:T(128)}) all-reduce(f32[]{:T(128)} %bitcast.1, f32[]{:T(128)S(6)} %convert_element_type.24), channel_id=1, replica_groups=mesh['dp'=4,'fsdp'=4,'tensor'=2] {'dp','fsdp'}, use_global_device_ids=true, to_apply=%region_0.0 | all-reduce | flops 2 | bytes 16 | tf_op jit(solution)/shard_map/psum | solution.py:48
  45.7 0.0 copy-start
  45.7 3.3 fusion.5
  49.1 2.8 copy.44
  51.9 0.1 fusion.11
  52.0 0.0 copy-done
  52.0 2.9 copy.45
  54.9 0.0 copy-done.4
  54.9 0.1 reshape.103
  55.0 16.2 %fusion.6 = f32[4,448,448,8]{2,1,3,0:T(8,128)} fusion(bf16[448,4,8,128]{3,2,1,0:T(8,128)(2,1)} %bitcast.53, bf16[448,4,128,1]{2,1,0,3:T(4,128)(2,1)S(1)} %bitcast.56), kind=kOutput, calls=%fused_computation.11 | convolution fusion | flops 1644167168 | bytes 29818880 | tf_op jit(solution)/shard_map/tkgd,skd->kgts/dot_general | solution.py:17
  71.3 29.3 %fusion.20 = (f32[4,8,448]{2,1,0:T(8,128)S(1)}, f32[4,8,448,448]{2,3,1,0:T(8,128)}) fusion(f32[4,448,448,8]{2,1,3,0:T(8,128)} %fusion.6, pred[448,448]{0,1:T(8,128)(4,1)S(1)} %fusion.11), kind=kOutput, calls=%fused_computation.36 | output fusion | flops 38535616 | bytes 51638272 | tf_op jit(solution)/shard_map/sub | solution.py:24
  100.6 17.7 %divide_convert_fusion = bf16[4,8,448,448]{2,3,1,0:T(8,128)(2,1)} fusion(f32[4,8,448,448]{2,3,1,0:T(8,128)} %get-tuple-element.27, f32[4,8,448]{2,1,0:T(8,128)S(1)} %get-tuple-element.26), kind=kLoop, calls=%fused_computation.2 | loop fusion | flops 12845056 | bytes 38592512 | tf_op jit(solution)/shard_map/convert_element_type | solution.py:25
  118.2 28.1 %copy.39 = bf16[4,8,448,448]{3,1,0,2:T(8,128)(2,1)} copy(bf16[4,8,448,448]{2,3,1,0:T(8,128)(2,1)} %divide_convert_fusion) | data formatting | bytes 25690112 | tf_op jit(solution)/shard_map/convert_element_type | solution.py:25
  146.3 11.0 %fusion.9 = bf16[4,56,8,128]{3,2,1,0:T(8,128)(2,1)S(1)} fusion(bf16[448,4,8,128]{3,2,1,0:T(8,128)(2,1)} %bitcast.52, bf16[4,8,448,448]{3,1,0,2:T(8,128)(2,1)} %copy.39), kind=kOutput, calls=%fused_computation.16 | convolution fusion | flops 1644396544 | bytes 16973824 | tf_op jit(solution)/shard_map/kgts,tkgd->skd/dot_general | solution.py:30
  157.2 11.2 %convolution_bitcast_fusion = f32[8192,512]{0,1:T(8,128)} fusion(bf16[448,8192]{1,0:T(8,128)(2,1)} %param.10, bf16[4,56,8,128]{3,2,1,0:T(8,128)(2,1)S(1)} %fusion.9), kind=kOutput, calls=%fused_computation.8 | convolution fusion | flops 3758096384 | bytes 24576000 | tf_op jit(solution)/shard_map/dot_general | solution.py:59
  168.4 0.0 copy-start.1
  168.4 0.0 copy-start.2
  168.5 0.0 copy-start.3
  168.5 0.0 copy-start.5
  168.5 0.0 reduce-scatter.2.cloned.1.call-update
  168.5 0.0 all-gather.2.cloned.1.call-start
  168.5 1.1 copy-done.1
  169.7 1.3 copy.25
  171.0 0.0 copy-done.2
  171.0 1.3 copy.30
  172.3 0.0 copy-done.3
  172.3 1.3 copy.32
  173.6 170.9 %reduce-scatter.2.cloned.1.call-done = f32[512,512]{0,1:T(8,128)} async-done(((f32[8192,512]{0,1:T(8,128)}), f32[512,512]{0,1:T(8,128)}) %reduce-scatter.2.cloned.1.call-update) | async-done | bytes 1048592 | tf_op jit(solution)/shard_map/reduce_scatter | solution.py:58
  344.5 3.8 %fusion.17 = (bf16[512,512]{0,1:T(8,128)(2,1)}, f32[512,512]{0,1:T(8,128)S(1)}, f32[512,512]{0,1:T(8,128)S(1)}, f32[512,512]{0,1:T(8,128)S(1)}) fusion(f32[512,512]{0,1:T(8,128)} %copy.32, f32[512,512]{0,1:T(8,128)} %reduce-scatter.2.cloned.1.call-done, f32[512,512]{0,1:T(8,128)} %copy.25, f32[512,512]{0,1:T(8,128)} %copy.30), kind=kLoop, calls=%fused_computation.34 | loop fusion | flops 4194304 | bytes 7864320 | tf_op jit(solution)/shard_map/convert_element_type | solution.py:70
  348.3 0.0 all-gather.2.cloned.1.call-update
  348.3 0.0 copy-done.5
  348.3 0.1 dynamic_slice.16
  348.4 0.7 fusion.19
  356.8 1.3 copy.34
  358.1 1.3 copy.35
  359.4 1.3 copy.36
  360.7 8.1 %all-gather.2.cloned.1.call-done = bf16[512,1024]{0,1:T(8,128)(2,1)} async-done(((bf16[512,512]{0,1:T(8,128)(2,1)}), bf16[512,1024]{0,1:T(8,128)(2,1)}) %all-gather.2.cloned.1.call-update) | async-done | bytes 1048592 | tf_op jit(solution)/shard_map/all_gather | solution.py:74
  368.8 1.1 dynamic-slice_select_fusion.3
  369.9 0.1 pad_maximum_fusion
  370.0 1.0 copy.42
  (2 shorter events, 0.0 us)
Async XLA Ops:
  7.2 47.7 %copy-start.4 = (bf16[448,512]{1,0:T(8,128)(2,1)S(1)}, bf16[448,512]{1,0:T(8,128)(2,1)}, u32[]{:S(2)}) copy-start(bf16[448,512]{1,0:T(8,128)(2,1)} %param.12) | copy-start | bytes 1376260
  7.2 337.3 %reduce-scatter.2.cloned.1.call-start = ((), (), s32[]{:S(2)}) async-start(), calls=%async_computation.1 | async-start | bytes 17825792 | tf_op jit(solution)/shard_map/reduce_scatter | solution.py:58
  45.7 6.3 %copy-start = (bf16[448,4096]{1,0:T(8,128)(2,1)S(1)}, bf16[448,4096]{1,0:T(8,128)(2,1)}, u32[]{:S(2)}) copy-start(bf16[448,4096]{1,0:T(8,128)(2,1)} %param.11) | copy-start | bytes 11010052
  168.4 1.2 copy-start.1
  168.4 2.5 copy-start.2
  168.5 3.8 %copy-start.3 = (f32[512,512]{1,0:T(8,128)S(1)}, f32[512,512]{1,0:T(8,128)}, u32[]{:S(2)}) copy-start(f32[512,512]{1,0:T(8,128)} %param.16) | copy-start | bytes 3145732
  168.5 179.9 %copy-start.5 = (s32[8]{0:T(128)S(1)}, s32[8]{0:T(128)}, u32[]{:S(2)}) copy-start(s32[8]{0:T(128)} %param.19) | copy-start | bytes 100
  168.5 200.3 %all-gather.2.cloned.1.call-start = ((), (), s32[]{:S(2)}) async-start(), calls=%async_computation.2 | async-start | bytes 1572864 | tf_op jit(solution)/shard_map/all_gather | solution.py:74
Sparse Core Ops, SparseCore 0:
  168.6 175.8 reduce-scatter.1
  348.4 20.2 all-gather.1
where the time goes:
time: 379 us; the launch traced here: 378 us
  waiting for transfers between devices  179 us (47%)
  other arithmetic  55.4 us (15%)
  local copies, waits for them, and re-layouts  44.6 us (12%)
  matrix products  38.4 us (10%)
  blocking collectives  35.8 us (9%)
  between operations  24.5 us (6%)
    reduce_scatter x1, waiting for transfers between devices, on_device(): lax.psum_scatter(lax.dot_general(hidden_in, value_gradient, (((0,), (0,))...  171 us
    psum x1, blocking collectives, on_device(): lax.psum((jnp.sum(rewards), jnp.sum(lengths).astype(jnp.float32)), ('dp',...  35.8 us
    sub x1, other arithmetic, value_grad(): expo = jnp.exp(scores - top)  29.3 us
    convert_element_type x1, local copies, waits for them, and re-layouts, value_grad(): probs = (expo / jnp.sum(expo, axis=-1, keepdims=True)).astype(jnp.bfloat16)  28.1 us
    convert_element_type x1, other arithmetic, value_grad(): probs = (expo / jnp.sum(expo, axis=-1, keepdims=True)).astype(jnp.bfloat16)  17.7 us
    dot_general x1, matrix products, value_grad(): jnp.einsum('tkgd,skd->kgts', query_head_rows, key_head_rows, preferred_el...  16.2 us
    unnamed x20, local copies, waits for them, and re-layouts  14.7 us
    dot_general x1, matrix products, on_device(): lax.dot_general(hidden_in, value_gradient, (((0,), (0,)), ((), ())), pref...  11.2 us
  transfers between devices with their start and end apart: 2, of which 2 were waited for; matrix products, arithmetic and copies ran while one was open for 2% of the time, Pallas kernels for 0%

commit v1 on v0

v1 whole, which is shorter than its diff:
```python
import functools
import math

import jax
import jax.numpy as jnp
from jax import lax
from jax.experimental import pallas as pl
from jax.experimental.pallas import tpu as pltpu
from jax.sharding import PartitionSpec as P

HEAD_SIZE = 128
QUERY_PER_VALUE = 8
AXES = ("dp", "fsdp")
MESH = pl.DeviceIdType.MESH
F32 = jnp.float32
BF16 = jnp.bfloat16


def log2_of(number):
    return number.bit_length() - 1


def adam(grad, moment, second, master):
    new_moment = 0.9 * moment + 0.1 * grad
    new_second = 0.95 * second + 0.05 * grad * grad
    corrected = new_moment / (1.0 - 0.9**10) / (jnp.sqrt(new_second / (1.0 - 0.95**10)) + 1e-08)
    return new_moment, new_second, master - 0.002 * (corrected + 0.1 * master)


def query_blocks(slots):
    blocks = []
    for start in range(0, slots, 256):
        size = min(256, slots - start)
        blocks.append((start, size, start + size))
    return blocks


def step_kernel(
    sizes,
    rewards_ref,
    lengths_ref,
    layout_ref,
    hidden_hbm,
    queries_hbm,
    keys_ref,
    outgrad_hbm,
    master_ref,
    moment_ref,
    second_ref,
    weight_out,
    moment_out,
    second_out,
    rollout_out,
    hidden,
    queries,
    outgrad,
    bias,
    value_acc,
    value_t,
    part,
    landed,
    heads_all,
    scalar_sent,
    scalar_landed,
    load_sem,
    rs_send,
    rs_recv,
    scalar_send,
    scalar_recv,
    swap_send,
    swap_recv,
):
    dp_count, fsdp_count, tensor_count = sizes
    dp, fsdp, tensor = (lax.axis_index(a) for a in ("dp", "fsdp", "tensor"))
    dp_bits, fsdp_bits = log2_of(dp_count), log2_of(fsdp_count)
    stages = dp_bits + fsdp_bits
    blocks = dp_count * fsdp_count
    slots = hidden_hbm.shape[0]
    rows = master_ref.shape[0]
    heads = keys_ref.shape[1] // HEAD_SIZE
    group = QUERY_PER_VALUE * HEAD_SIZE

    bits, partners = [], []
    for k in range(stages):
        name, index, shift = ("dp", dp, k) if k < dp_bits else ("fsdp", fsdp, k - dp_bits)
        bit = (index // (1 << shift)) % 2
        bits.append(bit)
        partners.append({name: index + (1 - 2 * bit) * (1 << shift)})
    peers = [{"tensor": (tensor + d) % tensor_count} for d in range(1, tensor_count)]

    loads = []
    for c in range(heads):
        columns = pl.ds(c * group, group)
        loads.append(
            [
                pltpu.make_async_copy(source.at[:, columns], target.at[:, columns], load_sem.at[2 * c + i])
                for i, (source, target) in enumerate(((queries_hbm, queries), (outgrad_hbm, outgrad)))
            ]
        )
    hidden_load = pltpu.make_async_copy(hidden_hbm, hidden, load_sem.at[2 * heads])
    for copy in loads[0]:
        copy.start()
    hidden_load.start()
    for pair in loads[1:]:
        for copy in pair:
            copy.start()

    barrier = pltpu.get_barrier_semaphore()
    for target in partners + peers:
        pl.semaphore_signal(barrier, inc=1, device_id=target, device_id_type=MESH)

    length = lengths_ref[0]
    own_reward = jnp.full((8, 128), rewards_ref[0], F32)
    own_length = jnp.full((8, 128), length, jnp.int32).astype(F32)
    tile_row = lax.broadcasted_iota(jnp.int32, (8, 128), 0)
    totals = jnp.where(tile_row == 0, own_reward, own_length)

    key_pos = lax.broadcasted_iota(jnp.int32, (slots, slots), 0)
    query_pos = lax.broadcasted_iota(jnp.int32, (slots, slots), 1)
    bias[...] = jnp.where((key_pos <= query_pos) & (key_pos < length), 0.0, -1e30).astype(F32)
    exponent = F32(math.log2(math.e) / math.sqrt(HEAD_SIZE))

    pl.semaphore_wait(barrier, stages + tensor_count - 1)

    def scalar_copy(k):
        return pltpu.make_async_remote_copy(
            src_ref=scalar_sent.at[k],
            dst_ref=scalar_landed.at[k],
            send_sem=scalar_send.at[k],
            recv_sem=scalar_recv.at[k],
            device_id=partners[k],
            device_id_type=MESH,
        )

    def query_head(c, j):
        offset = pl.multiple_of((c * QUERY_PER_VALUE + j) * HEAD_SIZE, HEAD_SIZE)
        columns = pl.ds(offset, HEAD_SIZE)
        for start, size, seen in query_blocks(slots):
            scores = lax.dot_general(
                keys_ref[:seen, c * HEAD_SIZE : (c + 1) * HEAD_SIZE],
                queries[start : start + size, columns],
                (((1,), (1,)), ((), ())),
                preferred_element_type=F32,
            )
            scores = scores + bias[:seen, start : start + size]
            top = jnp.max(scores, axis=0, keepdims=True)
            expo = jnp.exp2((scores - top) * exponent)
            total = jnp.sum(expo, axis=0, keepdims=True)
            slot = start + lax.broadcasted_iota(jnp.int32, (1, size), 1)
            inverse = jnp.where(slot < length, 1.0 / total, 0.0)
            probs = (expo * inverse).astype(BF16)
            value_acc[:seen, :] += jnp.dot(
                probs, outgrad[start : start + size, columns], preferred_element_type=F32
            )

    def attention(c, first, last):
        @pl.loop(first, last)
        def _(j):
            query_head(c, j)

    def rows_of(position):
        bit = [(position // (1 << (stages - 1 - k))) % 2 for k in range(stages)]
        dp_of = sum(bit[k] * (1 << k) for k in range(dp_bits))
        fsdp_of = sum(bit[dp_bits + k] * (1 << k) for k in range(fsdp_bits))
        return dp_of * fsdp_count + fsdp_of

    sent_at, kept_at, land_at, half_of = [], [], [], []
    base, landing = 0, 0
    for k in range(stages):
        half = blocks >> (k + 1)
        sent_at.append(base + (1 - bits[k]) * half)
        base = base + bits[k] * half
        kept_at.append(base)
        half_of.append(half)
        land_at.append(landing)
        landing += half

    def reduce_copy(k, c):
        return pltpu.make_async_remote_copy(
            src_ref=part.at[c, pl.ds(sent_at[k], half_of[k])],
            dst_ref=landed.at[c, pl.ds(land_at[k], half_of[k])],
            send_sem=rs_send.at[k, c],
            recv_sem=rs_recv.at[k, c],
            device_id=partners[k],
            device_id_type=MESH,
        )

    def multiply(c, begin, count):
        @pl.loop(0, count)
        def _(i):
            position = begin + i
            columns = pl.ds(pl.multiple_of(rows_of(position) * rows, 128), rows)
            part[c, position] = jnp.dot(
                value_t[...], hidden[:, columns], preferred_element_type=F32
            ).astype(BF16)

    def fold(k, c, begin, count):
        @pl.loop(0, count)
        def _(i):
            position = begin + i
            arrived = landed[c, land_at[k] + position - kept_at[k]]
            part[c, position] = (part[c, position].astype(F32) + arrived.astype(F32)).astype(BF16)

    def advance(k, c):
        reduce_copy(k, c).wait_recv()
        fold(k, c, sent_at[k + 1], half_of[k + 1])
        reduce_copy(k + 1, c).start()
        fold(k, c, kept_at[k + 1], half_of[k + 1])

    def swap_copy(d, c):
        return pltpu.make_async_remote_copy(
            src_ref=heads_all.at[c],
            dst_ref=heads_all.at[d * heads + c],
            send_sem=swap_send.at[d - 1, c],
            recv_sem=swap_recv.at[d - 1, c],
            device_id=peers[d - 1],
            device_id_type=MESH,
        )

    def finish(c):
        k = stages - 1
        reduce_copy(k, c).wait_recv()
        total = part[c, kept_at[k]].astype(F32) + landed[c, land_at[k]].astype(F32)
        columns = slice(c * HEAD_SIZE, (c + 1) * HEAD_SIZE)
        new_moment, new_second, weight = adam(
            total.T, moment_ref[:, columns], second_ref[:, columns], master_ref[:, columns]
        )
        heads_all[c] = weight.astype(BF16)
        for d in range(1, tensor_count):
            swap_copy(d, c).start()
        moment_out[:, columns] = new_moment
        second_out[:, columns] = new_second
        weight_out[:, columns] = weight

    share = -(-QUERY_PER_VALUE // stages)
    for c in range(heads):
        for copy in loads[c]:
            copy.wait()
        value_acc[...] = jnp.zeros_like(value_acc)
        if c == 0:
            done = 0
            for k in range(stages):
                scalar_sent[k] = totals
                scalar_copy(k).start()
                last = min(QUERY_PER_VALUE, done + share)
                attention(c, done, last)
                done = last
                scalar_copy(k).wait_recv()
                totals = totals + scalar_landed[k]
            if done < QUERY_PER_VALUE:
                attention(c, done, QUERY_PER_VALUE)
            count = F32(blocks)
            advantage = own_reward[:1] - totals[0:1] / count
            value_weight = advantage * count / totals[1:2]
            hidden_load.wait()
        else:
            attention(c, 0, QUERY_PER_VALUE)
            advance(0, c - 1)
        value_t[...] = (value_acc[...] * value_weight).T.astype(BF16)
        multiply(c, sent_at[0], half_of[0])
        reduce_copy(0, c).start()
        multiply(c, kept_at[0], half_of[0])
    advance(0, heads - 1)
    for step in range(heads + stages - 2):
        for k in reversed(range(1, stages)):
            c = step - (k - 1)
            if 0 <= c < heads:
                if k < stages - 1:
                    advance(k, c)
                else:
                    finish(c)

    for c in range(heads):
        for d in range(1, tensor_count):
            swap_copy(d, c).wait_recv()
    for c in range(heads):
        wanted = layout_ref[tensor * heads + c]
        back = (tensor - wanted // heads + tensor_count) % tensor_count
        rollout_out[:, c * HEAD_SIZE : (c + 1) * HEAD_SIZE] = heads_all[back * heads + wanted % heads]
    for k in range(stages):
        scalar_copy(k).wait_send()
        for c in range(heads):
            reduce_copy(k, c).wait_send()
    for c in range(heads):
        for d in range(1, tensor_count):
            swap_copy(d, c).wait_send()


def fused_step(
    sizes, hidden_in, queries, keys, output_gradient, rewards, lengths, master, moment, second, layout
):
    dp_count, fsdp_count, tensor_count = sizes
    blocks = dp_count * fsdp_count
    stages = log2_of(blocks)
    slots = hidden_in.shape[0]
    rows = master.shape[0]
    heads = keys.shape[1] // HEAD_SIZE
    smem = pl.BlockSpec(memory_space=pltpu.SMEM)
    vmem = pl.BlockSpec(memory_space=pltpu.VMEM)
    anywhere = pl.BlockSpec(memory_space=pl.ANY)
    dma = pltpu.SemaphoreType.DMA
    return pl.pallas_call(
        functools.partial(step_kernel, sizes),
        out_shape=[jax.ShapeDtypeStruct(master.shape, F32)] * 3
        + [jax.ShapeDtypeStruct(master.shape, BF16)],
        in_specs=[smem, smem, smem, anywhere, anywhere, vmem, anywhere, vmem, vmem, vmem],
        out_specs=[vmem] * 4,
        scratch_shapes=[
            pltpu.VMEM(hidden_in.shape, BF16),
            pltpu.VMEM(queries.shape, BF16),
            pltpu.VMEM(queries.shape, BF16),
            pltpu.VMEM((slots, slots), F32),
            pltpu.VMEM((slots, HEAD_SIZE), F32),
            pltpu.VMEM((HEAD_SIZE, slots), BF16),
            pltpu.VMEM((heads, blocks, HEAD_SIZE, rows), BF16),
            pltpu.VMEM((heads, blocks - 1, HEAD_SIZE, rows), BF16),
            pltpu.VMEM((tensor_count * heads, rows, HEAD_SIZE), BF16),
            pltpu.VMEM((stages, 8, 128), F32),
            pltpu.VMEM((stages, 8, 128), F32),
            dma((2 * heads + 1,)),
            dma((stages, heads)),
            dma((stages, heads)),
            dma((stages,)),
            dma((stages,)),
            dma((tensor_count - 1, heads)),
            dma((tensor_count - 1, heads)),
        ],
        compiler_params=pltpu.CompilerParams(
            collective_id=0, has_side_effects=True, vmem_limit_bytes=60 * 1024 * 1024
        ),
    )(rewards, lengths, layout, hidden_in, queries, keys, output_gradient, master, moment, second)


def value_grad(query_matrix, key_matrix, out_rows, value_weight, length):
    token_slot_index = query_matrix.shape[0]
    heads_local = key_matrix.shape[1] // HEAD_SIZE
    query_head_rows = query_matrix.reshape(
        token_slot_index, heads_local, QUERY_PER_VALUE, HEAD_SIZE
    )
    key_head_rows = key_matrix.reshape(token_slot_index, heads_local, HEAD_SIZE)
    scores = jnp.einsum(
        "tkgd,skd->kgts", query_head_rows, key_head_rows, preferred_element_type=jnp.float32
    ) / jnp.sqrt(jnp.float32(HEAD_SIZE))
    position = jnp.arange(token_slot_index)
    allowed = (position[None, :] <= position[:, None]) & (position[None, :] < length)
    scores = jnp.where(allowed[None, None], scores, jnp.float32(-1e30))
    top = jnp.max(scores, axis=-1, keepdims=True)
    expo = jnp.exp(scores - top)
    probs = (expo / jnp.sum(expo, axis=-1, keepdims=True)).astype(jnp.bfloat16)
    attention_gradient = (value_weight[:, None] * out_rows.astype(jnp.float32)).astype(jnp.bfloat16)
    head_gradient = attention_gradient.reshape(
        token_slot_index, heads_local, QUERY_PER_VALUE, HEAD_SIZE
    )
    value_gradient = jnp.einsum(
        "kgts,tkgd->skd", probs, head_gradient, preferred_element_type=jnp.float32
    )
    return value_gradient.reshape(token_slot_index, heads_local * HEAD_SIZE).astype(jnp.bfloat16)


def plain_step(
    hidden_in, queries, keys, output_gradient, rewards, lengths, master, moment, second, layout
):
    reward_sum, length_sum = lax.psum(
        (jnp.sum(rewards), jnp.sum(lengths).astype(jnp.float32)), AXES
    )
    seq_count = jnp.float32(lax.axis_size(AXES))
    advantage = rewards[0] - reward_sum / seq_count
    position = jnp.arange(hidden_in.shape[0])
    value_weight = jnp.where(
        position < lengths[0], advantage * seq_count / length_sum, jnp.float32(0.0)
    )
    value_gradient = value_grad(queries, keys, output_gradient, value_weight, lengths[0])
    grad = lax.psum_scatter(
        lax.dot_general(
            hidden_in, value_gradient, (((0,), (0,)), ((), ())), preferred_element_type=jnp.float32
        ),
        AXES,
        scatter_dimension=0,
        tiled=True,
    )
    new_moment, new_second, weight = adam(grad, moment, second, master)
    rounded = weight.astype(jnp.bfloat16)
    row_count = rounded.shape[0]
    heads_local = rounded.shape[1] // HEAD_SIZE
    targets = lax.dynamic_slice_in_dim(layout, lax.axis_index("tensor") * heads_local, heads_local)
    piece = lax.all_gather(rounded, "tensor", axis=1, tiled=True)
    piece_rows = piece.reshape(row_count, piece.shape[1] // HEAD_SIZE, HEAD_SIZE)
    rollout = jnp.take(piece_rows, targets, axis=1).reshape(row_count, heads_local * HEAD_SIZE)
    return weight, new_moment, new_second, rollout


def solution(mesh):
    sizes = tuple(mesh.shape[a] for a in ("dp", "fsdp", "tensor"))

    def on_device(hidden_in, *rest):
        rows = hidden_in.shape[1] // (sizes[0] * sizes[1])
        powers = all(size & (size - 1) == 0 for size in sizes[:2])
        if rows % 128 == 0 and powers and sizes[2] > 1:
            return tuple(fused_step(sizes, hidden_in, *rest))
        return plain_step(hidden_in, *rest)

    rows_spec, split_spec = P(AXES, None), P(AXES, "tensor")
    placed = (rows_spec,) + (split_spec,) * 3 + (P(AXES),) * 2 + (split_spec,) * 3 + (P(),)
    return jax.shard_map(
        on_device, mesh=mesh, in_specs=placed, out_specs=(split_spec,) * 4, check_vma=False
    )
```

time: 379 us -> 120 us (0.32)
  waiting for transfers between devices: 179 us -> 0 us
  Pallas kernels: 0 us -> 111 us
  other arithmetic: 55.4 us -> 0 us
  matrix products: 38.4 us -> 0 us
  local copies, waits for them, and re-layouts: 44.6 us -> 6.41 us
  blocking collectives: 35.8 us -> 0 us
  between operations: 24.5 us -> 1.95 us
    reduce_scatter x1 -> x0, waiting for transfers between devices: 171 us -> none  [on_device(): lax.psum_scatter(lax.dot_general(hidden_in, value_gradient, (((0,), (0,))...]
    pallas_call x0 -> x1, Pallas kernels: none -> 111 us  [fused_step(): pl.pallas_call(functools.partial(step_kernel, sizes), out_shape=[jax.Shap...]
    dot_general x3 -> x0, matrix products: 38.4 us -> none  [the longest x1 16.2 us: value_grad(): jnp.einsum('tkgd,skd->kgts', query_head_rows, key_head_rows, preferred_el...]
    psum x1 -> x0, blocking collectives: 35.8 us -> none  [on_device(): lax.psum((jnp.sum(rewards), jnp.sum(lengths).astype(jnp.float32)), ('dp',...]
    sub x1 -> x0, other arithmetic: 29.3 us -> none  [value_grad(): expo = jnp.exp(scores - top)]
    convert_element_type x1 -> x0, local copies, waits for them, and re-layouts: 28.1 us -> none  [value_grad(): probs = (expo / jnp.sum(expo, axis=-1, keepdims=True)).astype(jnp.bfloat16)]
    convert_element_type x2 -> x0, other arithmetic: 21.5 us -> none  [the longest x1 17.7 us: value_grad(): probs = (expo / jnp.sum(expo, axis=-1, keepdims=True)).astype(jnp.bfloat16)]
    unnamed x20 -> x8, local copies, waits for them, and re-layouts: 14.7 us -> 6.41 us
  transfers between devices with their start and end apart: 2 -> 0, of which waited for: 2 -> 0; matrix products, arithmetic and copies ran while one was open for 2% -> 0% of each run, Pallas kernels for 0% -> 0%
where the time goes in v1:
time: 120 us
  Pallas kernels  111 us (92%)
  local copies, waits for them, and re-layouts  6.41 us (5%)
  between operations  1.95 us (2%)
    pallas_call x1, Pallas kernels, fused_step(): pl.pallas_call(functools.partial(step_kernel, sizes), out_shape=[jax.Shap...  111 us
    unnamed x8, local copies, waits for them, and re-layouts  6.41 us

profile of v1, /device:TPU:0, one launch (start us, length us, event | category | flops | bytes accessed | tf_op | source)
XLA Modules:
  0.0 119.8 jit_solution(13054616937651483231)
XLA Ops:
  1.9 111.5 %shard_map.129 = (f32[512,512]{1,0:T(8,128)}, f32[512,512]{1,0:T(8,128)}, f32[512,512]{1,0:T(8,128)}, bf16[512,512]{1,0:T(8,128)(2,1)}) custom-call(f32[1]{0:T(128)S(6)} %copy.18.rewards_ref, s32[1]{0:T(128)S(6)} %copy.19.lengths_ref, s32[8]{0:T(128)} %layout_ref.1, bf16[448,8192]{1,0:T(8,128)(2,1)} %hidden_hbm.1, bf16[448,4096]{1,0:T(8,128)(2,1)} %queries_hbm.1, ...), custom_call_target="tpu_custom_call" | custom-call | tf_op jit(solution)/shard_map/pallas_call | solution.py:302
  113.4 0.0 copy-start
  113.4 0.0 copy-start.1
  113.4 2.4 %copy.20 = f32[512,512]{1,0:T(8,128)} copy(f32[512,512]{1,0:T(8,128)} %get-tuple-element.8) | data formatting | bytes 2097152
  115.8 2.3 %copy.21 = f32[512,512]{1,0:T(8,128)} copy(f32[512,512]{1,0:T(8,128)} %get-tuple-element.9) | data formatting | bytes 2097152
  118.1 0.0 copy-done
  118.1 1.0 copy.22
  119.0 0.0 copy-done.1
  119.0 0.8 copy.23
Async XLA Ops:
  113.4 4.7 %copy-start = (f32[512,512]{1,0:T(8,128)S(1)}, f32[512,512]{1,0:T(8,128)}, u32[]{:S(2)}) copy-start(f32[512,512]{1,0:T(8,128)} %get-tuple-element.10) | copy-start | bytes 3145732
  113.4 5.6 %copy-start.1 = (bf16[512,512]{1,0:T(8,128)(2,1)S(1)}, bf16[512,512]{1,0:T(8,128)(2,1)}, u32[]{:S(2)}) copy-start(bf16[512,512]{1,0:T(8,128)(2,1)} %get-tuple-element.11) | copy-start | bytes 1572868

commit v2 on v1

--- a/solution.py
+++ b/solution.py
@@ -44,16 +44,17 @@
     queries_hbm,
     keys_ref,
     outgrad_hbm,
-    master_ref,
-    moment_ref,
-    second_ref,
-    weight_out,
-    moment_out,
-    second_out,
+    master_hbm,
+    moment_hbm,
+    second_hbm,
+    grad_out,
     rollout_out,
     hidden,
     queries,
     outgrad,
+    master_ref,
+    moment_ref,
+    second_ref,
     bias,
     value_acc,
     value_t,
@@ -86,6 +87,10 @@
         bit = (index // (1 << shift)) % 2
         bits.append(bit)
         partners.append({name: index + (1 - 2 * bit) * (1 << shift)})
+    others = [
+        [{name: (index + d) % size} for d in range(1, size)]
+        for name, index, size in (("dp", dp, dp_count), ("fsdp", fsdp, fsdp_count))
+    ]
     peers = [{"tensor": (tensor + d) % tensor_count} for d in range(1, tensor_count)]
 
     loads = []
@@ -104,9 +109,17 @@
     for pair in loads[1:]:
         for copy in pair:
             copy.start()
+    state_loads = [
+        pltpu.make_async_copy(source, target, load_sem.at[2 * heads + 1 + i])
+        for i, (source, target) in enumerate(
+            ((master_hbm, master_ref), (moment_hbm, moment_ref), (second_hbm, second_ref))
+        )
+    ]
+    for copy in state_loads:
+        copy.start()
 
     barrier = pltpu.get_barrier_semaphore()
-    for target in partners + peers:
+    for target in others[0] + others[1] + peers:
         pl.semaphore_signal(barrier, inc=1, device_id=target, device_id_type=MESH)
 
     length = lengths_ref[0]
@@ -120,17 +133,31 @@
     bias[...] = jnp.where((key_pos <= query_pos) & (key_pos < length), 0.0, -1e30).astype(F32)
     exponent = F32(math.log2(math.e) / math.sqrt(HEAD_SIZE))
 
-    pl.semaphore_wait(barrier, stages + tensor_count - 1)
-
-    def scalar_copy(k):
-        return pltpu.make_async_remote_copy(
-            src_ref=scalar_sent.at[k],
-            dst_ref=scalar_landed.at[k],
-            send_sem=scalar_send.at[k],
-            recv_sem=scalar_recv.at[k],
-            device_id=partners[k],
-            device_id_type=MESH,
-        )
+    def scalar_copies(turn):
+        first = turn * (dp_count - 1)
+        return [
+            pltpu.make_async_remote_copy(
+                src_ref=scalar_sent.at[turn],
+                dst_ref=scalar_landed.at[first + i],
+                send_sem=scalar_send.at[first + i],
+                recv_sem=scalar_recv.at[first + i],
+                device_id=target,
+                device_id_type=MESH,
+            )
+            for i, target in enumerate(others[turn])
+        ]
+
+    def send_scalars(turn, tile):
+        scalar_sent[turn] = tile
+        for copy in scalar_copies(turn):
+            copy.start()
+
+    def add_scalars(turn, tile):
+        first = turn * (dp_count - 1)
+        for i, copy in enumerate(scalar_copies(turn)):
+            copy.wait_recv()
+            tile = tile + scalar_landed[first + i]
+        return tile
 
     def query_head(c, j):
         offset = pl.multiple_of((c * QUERY_PER_VALUE + j) * HEAD_SIZE, HEAD_SIZE)
@@ -149,12 +176,12 @@
             slot = start + lax.broadcasted_iota(jnp.int32, (1, size), 1)
             inverse = jnp.where(slot < length, 1.0 / total, 0.0)
             probs = (expo * inverse).astype(BF16)
-            value_acc[:seen, :] += jnp.dot(
+            value_acc[c, :seen, :] += jnp.dot(
                 probs, outgrad[start : start + size, columns], preferred_element_type=F32
             )
 
     def attention(c, first, last):
-        @pl.loop(first, last)
+        @pl.loop(first, last, unroll=True)
         def _(j):
             query_head(c, j)
 
@@ -175,12 +202,12 @@
         land_at.append(landing)
         landing += half
 
-    def reduce_copy(k, c):
+    def reduce_copy(k, u):
         return pltpu.make_async_remote_copy(
-            src_ref=part.at[c, pl.ds(sent_at[k], half_of[k])],
-            dst_ref=landed.at[c, pl.ds(land_at[k], half_of[k])],
-            send_sem=rs_send.at[k, c],
-            recv_sem=rs_recv.at[k, c],
+            src_ref=part.at[u, pl.ds(sent_at[k], half_of[k])],
+            dst_ref=landed.at[u, pl.ds(land_at[k], half_of[k])],
+            send_sem=rs_send.at[k, u],
+            recv_sem=rs_recv.at[k, u],
             device_id=partners[k],
             device_id_type=MESH,
         )
@@ -190,22 +217,24 @@
         def _(i):
             position = begin + i
             columns = pl.ds(pl.multiple_of(rows_of(position) * rows, 128), rows)
-            part[c, position] = jnp.dot(
+            product = jnp.dot(
                 value_t[...], hidden[:, columns], preferred_element_type=F32
             ).astype(BF16)
-
-    def fold(k, c, begin, count):
+            part[2 * c, position] = product[: HEAD_SIZE // 2]
+            part[2 * c + 1, position] = product[HEAD_SIZE // 2 :]
+
+    def fold(k, u, begin, count):
         @pl.loop(0, count)
         def _(i):
             position = begin + i
-            arrived = landed[c, land_at[k] + position - kept_at[k]]
-            part[c, position] = (part[c, position].astype(F32) + arrived.astype(F32)).astype(BF16)
-
-    def advance(k, c):
-        reduce_copy(k, c).wait_recv()
-        fold(k, c, sent_at[k + 1], half_of[k + 1])
-        reduce_copy(k + 1, c).start()
-        fold(k, c, kept_at[k + 1], half_of[k + 1])
+            arrived = landed[u, land_at[k] + position - kept_at[k]]
+            part[u, position] = (part[u, position].astype(F32) + arrived.astype(F32)).astype(BF16)
+
+    def advance(k, u):
+        reduce_copy(k, u).wait_recv()
+        fold(k, u, sent_at[k + 1], half_of[k + 1])
+        reduce_copy(k + 1, u).start()
+        fold(k, u, kept_at[k + 1], half_of[k + 1])
 
     def swap_copy(d, c):
         return pltpu.make_async_remote_copy(
@@ -217,58 +246,72 @@
             device_id_type=MESH,
         )
 
+    def arrive(u):
+        k = stages - 1
+        reduce_copy(k, u).wait_recv()
+        return part[u, kept_at[k]].astype(F32) + landed[u, land_at[k]].astype(F32)
+
     def finish(c):
-        k = stages - 1
-        reduce_copy(k, c).wait_recv()
-        total = part[c, kept_at[k]].astype(F32) + landed[c, land_at[k]].astype(F32)
+        total = jnp.concatenate([arrive(2 * c), arrive(2 * c + 1)], axis=0).T
         columns = slice(c * HEAD_SIZE, (c + 1) * HEAD_SIZE)
-        new_moment, new_second, weight = adam(
-            total.T, moment_ref[:, columns], second_ref[:, columns], master_ref[:, columns]
+        _, _, weight = adam(
+            total, moment_ref[:, columns], second_ref[:, columns], master_ref[:, columns]
         )
         heads_all[c] = weight.astype(BF16)
         for d in range(1, tensor_count):
             swap_copy(d, c).start()
-        moment_out[:, columns] = new_moment
-        second_out[:, columns] = new_second
-        weight_out[:, columns] = weight
-
-    share = -(-QUERY_PER_VALUE // stages)
+        grad_out[:, columns] = total
+
+    def attend(c, first=0, last=QUERY_PER_VALUE):
+        if first == 0:
+            for copy in loads[c]:
+                copy.wait()
+            value_acc[c] = jnp.zeros((slots, HEAD_SIZE), F32)
+        attention(c, first, last)
+
+    attend(0, 0, 4)
+    pl.semaphore_wait(barrier, dp_count + fsdp_count + tensor_count - 3)
+    send_scalars(0, totals)
+    attend(0, 4, QUERY_PER_VALUE)
+    totals = add_scalars(0, totals)
+    send_scalars(1, totals)
+    attend(1)
+    totals = add_scalars(1, totals)
+    count = F32(blocks)
+    value_weight = (own_reward[:1] - totals[0:1] / count) * count / totals[1:2]
+    hidden_load.wait()
+
+    pending = {u: 0 for u in range(2 * heads)}
+
+    def advance_head(k, c):
+        for u in (2 * c, 2 * c + 1):
+            advance(k, u)
+            pending[u] = k + 1
+
     for c in range(heads):
-        for copy in loads[c]:
-            copy.wait()
-        value_acc[...] = jnp.zeros_like(value_acc)
-        if c == 0:
-            done = 0
-            for k in range(stages):
-                scalar_sent[k] = totals
-                scalar_copy(k).start()
-                last = min(QUERY_PER_VALUE, done + share)
-                attention(c, done, last)
-                done = last
-                scalar_copy(k).wait_recv()
-                totals = totals + scalar_landed[k]
-            if done < QUERY_PER_VALUE:
-                attention(c, done, QUERY_PER_VALUE)
-            count = F32(blocks)
-            advantage = own_reward[:1] - totals[0:1] / count
-            value_weight = advantage * count / totals[1:2]
-            hidden_load.wait()
-        else:
-            attention(c, 0, QUERY_PER_VALUE)
-            advance(0, c - 1)
-        value_t[...] = (value_acc[...] * value_weight).T.astype(BF16)
-        multiply(c, sent_at[0], half_of[0])
-        reduce_copy(0, c).start()
-        multiply(c, kept_at[0], half_of[0])
-    advance(0, heads - 1)
-    for step in range(heads + stages - 2):
+        value_t[...] = (value_acc[c] * value_weight).T.astype(BF16)
+        for begin in (sent_at[0], kept_at[0]):
+            multiply(c, begin, half_of[0])
+            if begin is sent_at[0]:
+                reduce_copy(0, 2 * c).start()
+                reduce_copy(0, 2 * c + 1).start()
+        advance_head(0, c)
+        if c + 2 < heads:
+            attend(c + 2)
+        if 0 < c < heads - 1:
+            advance_head(1, c - 1)
+        elif c == heads - 1:
+            advance_head(2, 0)
+    for copy in state_loads:
+        copy.wait()
+    for step in range(2 * heads + stages - 2):
         for k in reversed(range(1, stages)):
-            c = step - (k - 1)
-            if 0 <= c < heads:
+            u = step - (k - 1)
+            if 0 <= u < 2 * heads and pending[u] <= k:
                 if k < stages - 1:
-                    advance(k, c)
-                else:
-                    finish(c)
+                    advance(k, u)
+                elif u % 2 == 1:
+                    finish(u // 2)
 
     for c in range(heads):
         for d in range(1, tensor_count):
@@ -278,9 +321,10 @@
         back = (tensor - wanted // heads + tensor_count) % tensor_count
         rollout_out[:, c * HEAD_SIZE : (c + 1) * HEAD_SIZE] = heads_all[back * heads + wanted % heads]
     for k in range(stages):
-        scalar_copy(k).wait_send()
-        for c in range(heads):
-            reduce_copy(k, c).wait_send()
+        for u in range(2 * heads):
+            reduce_copy(k, u).wait_send()
+    for copy in scalar_copies(0) + scalar_copies(1):
+        copy.wait_send()
     for c in range(heads):
         for d in range(1, tensor_count):
             swap_copy(d, c).wait_send()
@@ -299,29 +343,34 @@
     vmem = pl.BlockSpec(memory_space=pltpu.VMEM)
     anywhere = pl.BlockSpec(memory_space=pl.ANY)
     dma = pltpu.SemaphoreType.DMA
-    return pl.pallas_call(
+    grad, rollout = pl.pallas_call(
         functools.partial(step_kernel, sizes),
-        out_shape=[jax.ShapeDtypeStruct(master.shape, F32)] * 3
-        + [jax.ShapeDtypeStruct(master.shape, BF16)],
-        in_specs=[smem, smem, smem, anywhere, anywhere, vmem, anywhere, vmem, vmem, vmem],
-        out_specs=[vmem] * 4,
+        out_shape=[
+            jax.ShapeDtypeStruct(master.shape, F32),
+            jax.ShapeDtypeStruct(master.shape, BF16),
+        ],
+        in_specs=[smem] * 3 + [anywhere, anywhere, vmem] + [anywhere] * 4,
+        out_specs=[vmem] * 2,
         scratch_shapes=[
             pltpu.VMEM(hidden_in.shape, BF16),
             pltpu.VMEM(queries.shape, BF16),
             pltpu.VMEM(queries.shape, BF16),
+            pltpu.VMEM(master.shape, F32),
+            pltpu.VMEM(master.shape, F32),
+            pltpu.VMEM(master.shape, F32),
             pltpu.VMEM((slots, slots), F32),
-            pltpu.VMEM((slots, HEAD_SIZE), F32),
+            pltpu.VMEM((heads, slots, HEAD_SIZE), F32),
             pltpu.VMEM((HEAD_SIZE, slots), BF16),
-            pltpu.VMEM((heads, blocks, HEAD_SIZE, rows), BF16),
-            pltpu.VMEM((heads, blocks - 1, HEAD_SIZE, rows), BF16),
+            pltpu.VMEM((2 * heads, blocks, HEAD_SIZE // 2, rows), BF16),
+            pltpu.VMEM((2 * heads, blocks - 1, HEAD_SIZE // 2, rows), BF16),
             pltpu.VMEM((tensor_count * heads, rows, HEAD_SIZE), BF16),
-            pltpu.VMEM((stages, 8, 128), F32),
-            pltpu.VMEM((stages, 8, 128), F32),
-            dma((2 * heads + 1,)),
-            dma((stages, heads)),
-            dma((stages, heads)),
-            dma((stages,)),
-            dma((stages,)),
+            pltpu.VMEM((2, 8, 128), F32),
+            pltpu.VMEM((dp_count + fsdp_count - 2, 8, 128), F32),
+            dma((2 * heads + 4,)),
+            dma((stages, 2 * heads)),
+            dma((stages, 2 * heads)),
+            dma((dp_count + fsdp_count - 2,)),
+            dma((dp_count + fsdp_count - 2,)),
             dma((tensor_count - 1, heads)),
             dma((tensor_count - 1, heads)),
         ],
@@ -329,6 +378,8 @@
             collective_id=0, has_side_effects=True, vmem_limit_bytes=60 * 1024 * 1024
         ),
     )(rewards, lengths, layout, hidden_in, queries, keys, output_gradient, master, moment, second)
+    new_moment, new_second, weight = adam(grad, moment, second, master)
+    return weight, new_moment, new_second, rollout
 
 
 def value_grad(query_matrix, key_matrix, out_rows, value_weight, length):
@@ -395,7 +446,9 @@
     def on_device(hidden_in, *rest):
         rows = hidden_in.shape[1] // (sizes[0] * sizes[1])
         powers = all(size & (size - 1) == 0 for size in sizes[:2])
-        if rows % 128 == 0 and powers and sizes[2] > 1:
+        heads = rest[1].shape[1] // HEAD_SIZE
+        large = heads > 1 and sizes[0] * sizes[1] >= 16 and min(sizes) > 1
+        if rows % 128 == 0 and powers and large:
             return tuple(fused_step(sizes, hidden_in, *rest))
         return plain_step(hidden_in, *rest)
 

time: 120 us -> 96.7 us (0.81)
  Pallas kernels: 111 us -> 90.3 us
  local copies, waits for them, and re-layouts: 6.41 us -> 0.81 us
  other arithmetic: 0 us -> 3.52 us
    pallas_call x1, Pallas kernels: 111 us -> 90.3 us  [fused_step(): pl.pallas_call(functools.partial(step_kernel, sizes), out_shape=[jax.Shap...]
    unnamed x8 -> x9, local copies, waits for them, and re-layouts: 6.41 us -> 0.81 us
    sub x0 -> x1, other arithmetic: none -> 3.52 us  [adam(): return (new_moment, new_second, master - 0.002 * (corrected + 0.1 * master))]
where the time goes in v2:
time: 96.7 us; the launch traced here: 96.6 us
  Pallas kernels  90.3 us (93%)
  other arithmetic  3.52 us (4%)
  between operations  1.99 us (2%)
    pallas_call x1, Pallas kernels, fused_step(): pl.pallas_call(functools.partial(step_kernel, sizes), out_shape=[jax.Shap...  90.3 us
    sub x1, other arithmetic, adam(): return (new_moment, new_second, master - 0.002 * (corrected + 0.1 * master))  3.52 us

profile of v2, /device:TPU:0, one launch (start us, length us, event | category | flops | bytes accessed | tf_op | source)
XLA Modules:
  0.0 96.6 jit_solution(15969106969981298293)
XLA Ops:
  1.9 0.0 copy-start
  1.9 0.0 copy-start.1
  1.9 0.0 copy-start.2
  2.0 90.3 %shard_map.129 = (f32[512,512]{1,0:T(8,128)}, bf16[512,512]{1,0:T(8,128)(2,1)}) custom-call(f32[1]{0:T(128)S(6)} %copy.15.rewards_ref, s32[1]{0:T(128)S(6)} %copy.16.lengths_ref, s32[8]{0:T(128)} %layout_ref.1, bf16[448,8192]{1,0:T(8,128)(2,1)} %hidden_hbm.1, bf16[448,4096]{1,0:T(8,128)(2,1)} %queries_hbm.1, bf16[448,512]{1,0:T(8,128)(2,1)} %keys_ref.1, ...), custom_call_target="tpu_custom_call" | custom-call | tf_op jit(solution)/shard_map/pallas_call | solution.py:346
  92.2 0.0 copy-done
  92.2 0.0 copy-done.1
  92.2 0.0 copy-done.2
  92.2 0.0 copy-start.3
  92.3 3.5 %multiply_subtract_fusion = (f32[512,512]{1,0:T(8,128)}, f32[512,512]{1,0:T(8,128)}, f32[512,512]{1,0:T(8,128)}) fusion(f32[512,512]{1,0:T(8,128)S(1)} %copy-done, f32[512,512]{1,0:T(8,128)} %get-tuple-element.6, f32[512,512]{1,0:T(8,128)S(1)} %copy-done.1, f32[512,512]{1,0:T(8,128)S(1)} %copy-done.2), kind=kLoop, calls=%fused_computation.2 | loop fusion | flops 3932160 | bytes 7340032 | tf_op jit(solution)/shard_map/sub | solution.py:27
  95.8 0.0 copy-done.3
  95.8 0.8 copy.17
Async XLA Ops:
  1.9 90.3 %copy-start = (f32[512,512]{1,0:T(8,128)S(1)}, f32[512,512]{1,0:T(8,128)}, u32[]{:S(2)}) copy-start(f32[512,512]{1,0:T(8,128)} %master_hbm.1) | copy-start | bytes 3145732
  1.9 90.3 %copy-start.1 = (f32[512,512]{1,0:T(8,128)S(1)}, f32[512,512]{1,0:T(8,128)}, u32[]{:S(2)}) copy-start(f32[512,512]{1,0:T(8,128)} %moment_hbm.1) | copy-start | bytes 3145732
  1.9 90.3 %copy-start.2 = (f32[512,512]{1,0:T(8,128)S(1)}, f32[512,512]{1,0:T(8,128)}, u32[]{:S(2)}) copy-start(f32[512,512]{1,0:T(8,128)} %second_hbm.1) | copy-start | bytes 3145732
  92.2 3.5 %copy-start.3 = (bf16[512,512]{1,0:T(8,128)(2,1)S(1)}, bf16[512,512]{1,0:T(8,128)(2,1)}, u32[]{:S(2)}) copy-start(bf16[512,512]{1,0:T(8,128)(2,1)} %get-tuple-element.18) | copy-start | bytes 1572868

commit v3 on v2

--- a/solution.py
+++ b/solution.py
@@ -213,7 +213,7 @@
         )
 
     def multiply(c, begin, count):
-        @pl.loop(0, count)
+        @pl.loop(0, count, unroll=2 if count % 2 == 0 else 1)
         def _(i):
             position = begin + i
             columns = pl.ds(pl.multiple_of(rows_of(position) * rows, 128), rows)
@@ -224,7 +224,7 @@
             part[2 * c + 1, position] = product[HEAD_SIZE // 2 :]
 
     def fold(k, u, begin, count):
-        @pl.loop(0, count)
+        @pl.loop(0, count, unroll=2 if count % 2 == 0 else 1)
         def _(i):
             position = begin + i
             arrived = landed[u, land_at[k] + position - kept_at[k]]

time: 96.7 us -> 95.2 us (0.984)
  Pallas kernels: 90.3 us -> 88.7 us
    pallas_call x1, Pallas kernels: 90.3 us -> 88.7 us  [fused_step(): pl.pallas_call(functools.partial(step_kernel, sizes), out_shape=[jax.Shap...]
where the time goes in v3:
time: 95.2 us; the launch traced here: 95 us
  Pallas kernels  88.7 us (93%)
  other arithmetic  3.52 us (4%)
  between operations  1.99 us (2%)
    pallas_call x1, Pallas kernels, fused_step(): pl.pallas_call(functools.partial(step_kernel, sizes), out_shape=[jax.Shap...  88.7 us
    sub x1, other arithmetic, adam(): return (new_moment, new_second, master - 0.002 * (corrected + 0.1 * master))  3.52 us

profile of v3, /device:TPU:0, one launch (start us, length us, event | category | flops | bytes accessed | tf_op | source)
XLA Modules:
  0.0 95.0 jit_solution(11792777065472224447)
XLA Ops:
  1.9 0.0 copy-start
  1.9 0.0 copy-start.1
  1.9 0.0 copy-start.2
  2.0 88.7 %shard_map.129 = (f32[512,512]{1,0:T(8,128)}, bf16[512,512]{1,0:T(8,128)(2,1)}) custom-call(f32[1]{0:T(128)S(6)} %copy.15.rewards_ref, s32[1]{0:T(128)S(6)} %copy.16.lengths_ref, s32[8]{0:T(128)} %layout_ref.1, bf16[448,8192]{1,0:T(8,128)(2,1)} %hidden_hbm.1, bf16[448,4096]{1,0:T(8,128)(2,1)} %queries_hbm.1, bf16[448,512]{1,0:T(8,128)(2,1)} %keys_ref.1, ...), custom_call_target="tpu_custom_call" | custom-call | tf_op jit(solution)/shard_map/pallas_call | solution.py:346
  90.7 0.0 copy-done
  90.7 0.0 copy-done.1
  90.7 0.0 copy-done.2
  90.7 0.0 copy-start.3
  90.7 3.5 %multiply_subtract_fusion = (f32[512,512]{1,0:T(8,128)}, f32[512,512]{1,0:T(8,128)}, f32[512,512]{1,0:T(8,128)}) fusion(f32[512,512]{1,0:T(8,128)S(1)} %copy-done, f32[512,512]{1,0:T(8,128)} %get-tuple-element.6, f32[512,512]{1,0:T(8,128)S(1)} %copy-done.1, f32[512,512]{1,0:T(8,128)S(1)} %copy-done.2), kind=kLoop, calls=%fused_computation.2 | loop fusion | flops 3932160 | bytes 7340032 | tf_op jit(solution)/shard_map/sub | solution.py:27
  94.2 0.0 copy-done.3
  94.2 0.8 copy.17
Async XLA Ops:
  1.9 88.8 %copy-start = (f32[512,512]{1,0:T(8,128)S(1)}, f32[512,512]{1,0:T(8,128)}, u32[]{:S(2)}) copy-start(f32[512,512]{1,0:T(8,128)} %master_hbm.1) | copy-start | bytes 3145732
  1.9 88.8 %copy-start.1 = (f32[512,512]{1,0:T(8,128)S(1)}, f32[512,512]{1,0:T(8,128)}, u32[]{:S(2)}) copy-start(f32[512,512]{1,0:T(8,128)} %moment_hbm.1) | copy-start | bytes 3145732
  1.9 88.8 %copy-start.2 = (f32[512,512]{1,0:T(8,128)S(1)}, f32[512,512]{1,0:T(8,128)}, u32[]{:S(2)}) copy-start(f32[512,512]{1,0:T(8,128)} %second_hbm.1) | copy-start | bytes 3145732
  90.7 3.5 %copy-start.3 = (bf16[512,512]{1,0:T(8,128)(2,1)S(1)}, bf16[512,512]{1,0:T(8,128)(2,1)}, u32[]{:S(2)}) copy-start(bf16[512,512]{1,0:T(8,128)(2,1)} %get-tuple-element.18) | copy-start | bytes 1572868
